TPU v7x, 128 devices: a whole 4x4x4 slice. The times are simulated.
128 devices in a mesh: group: 16 (over x, z_hi, core), inner: 8 (over z_lo, y).
Axes of the slice: x: 4, y: 4, z: 4 (z_hi: 2, z_lo: 2; z = z_hi * 2 + z_lo), core: 2. Of those that a mesh axis runs over, the one named last changes fastest.
Arguments:
- tokens: bfloat16 [16, 512, 2304], P('group', 'inner'), may hold values from -6 to 6
- lengths: int32 [16], P('group'), may hold values from 1 to 512, 5120 in all
- tenant_cut: int32 [16], P('group'), may hold values from 64 to 255
- expert_ids: int32 [16, 512, 2], P('group', 'inner'), may hold values from 0 to 7, all different within a row; in each aligned block of 64 rows (0 to 63, 64 to 127, ..., all dimensions but the last counted through in order) at most 20 rows name the same one
- trainer_qkv: float32 [2304, 3, 2048], P(('group', 'inner')), may hold values from -0.26 to 0.26
- trainer_gate_up: float32 [8, 2304, 2, 5760], P(None, ('group', 'inner')), may hold values from -0.125 to 0.125
- out_weight: bfloat16 [2048, 2304], P('inner'), may hold values from -0.75 to 0.75
- down_weight: bfloat16 [8, 5760, 2304], P('inner', 'group'), may hold values from -0.078125 to 0.078125
- attn_gain: float32 [2304], replicated, may hold values from 0.1 to 1.9
- moe_gain: float32 [2304], replicated, may hold values from 0.1 to 1.9
- router: bfloat16 [2304, 8], replicated, may hold values from -0.375 to 0.375
Outputs:
- server_qkv: bfloat16 [2304, 3, 2048], P(None, None, 'inner')
- server_gate_up: bfloat16 [8, 2304, 2, 5760], P('inner', None, None, 'group')
- layer_out: bfloat16 [16, 512, 2304], P('group', 'inner')
Inputs may be any that keep to these rules, and one draw needn't show every extreme that they name: `expert_ids`: in each aligned block of 64 token slots (the slots of one device) no expert is named more than 20 times, a bound that some block reaches. The two experts of a slot differ. `lengths`: some prompt uses all 512 slots.
All inputs are finite; a program needn't handle non-finite values. No bound on the sum of `lengths` on one device may be relied on, other than what follows from the above.
Results may differ from a plain program's by a relative error of at most 0.015.
Values may be sent and summed in bfloat16 or wider, within the bound.
A program may use at most 128 MiB of HBM per device.

v0:
```python
import math

import jax
import jax.numpy as jnp
from jax import lax
from jax.sharding import PartitionSpec as P

D = 2304
HEAD_DIM = 64
TOPK = 2


NORM_EPS = 1e-05
MASKED = -1e30


def rms_scaled(values, gain_row):
    mean_square = jnp.mean(values * values, axis=-1, keepdims=True)
    return values * lax.rsqrt(mean_square + NORM_EPS) * gain_row


def token_layout(length, cut_point, total):
    places = jnp.arange(total, dtype=jnp.int32)
    beyond = places >= length
    second = places >= cut_point
    starts = jnp.where(beyond, length, jnp.where(second, cut_point, 0))
    tenants = jnp.where(beyond, 2, jnp.where(second, 1, 0))
    return (places - starts, tenants, places)


def rotate_heads(values, positions):
    half_dim = values.shape[-1] // 2
    freqs = jnp.exp(-math.log(10000.0) * jnp.arange(half_dim, dtype=jnp.float32) / half_dim)
    angles = positions.astype(jnp.float32)[:, None] * freqs[None, :]
    cosine = jnp.cos(angles)[:, None, :]
    sine = jnp.sin(angles)[:, None, :]
    first_half = values[..., :half_dim]
    second_half = values[..., half_dim:]
    return jnp.concatenate(
        [first_half * cosine - second_half * sine, second_half * cosine + first_half * sine],
        axis=-1,
    )


def body(
    tokens,
    lengths,
    tenant_cut,
    expert_ids,
    trainer_qkv,
    trainer_gate_up,
    out_weight,
    down_weight,
    attn_gain,
    moe_gain,
    router,
):
    group_size = lax.axis_size("group")
    inner_size = lax.axis_size("inner")
    row_share = trainer_qkv.shape[0]
    head_block = trainer_qkv.shape[2] // inner_size
    cast_qkv = trainer_qkv.astype(jnp.bfloat16).reshape(row_share, 3, inner_size, head_block)
    head_parts = lax.all_to_all(cast_qkv, "inner", split_axis=2, concat_axis=0, tiled=True)
    head_parts = head_parts.reshape(inner_size * row_share, 3, head_block)
    server_qkv = lax.all_gather(head_parts, "group", axis=0, tiled=True)
    expert_count = trainer_gate_up.shape[0]
    local_experts = expert_count // inner_size
    hidden_share = trainer_gate_up.shape[3] // group_size
    cast_gate_up = trainer_gate_up.astype(jnp.bfloat16).reshape(
        inner_size, local_experts, row_share, 2, group_size, hidden_share
    )
    ordered = jnp.transpose(cast_gate_up, (4, 0, 1, 2, 3, 5))
    joined = ordered.reshape(group_size * inner_size, local_experts, 1, row_share, 2, hidden_share)
    moved = lax.all_to_all(joined, ("group", "inner"), split_axis=0, concat_axis=2, tiled=True)
    server_gate_up = moved.reshape(local_experts, D, 2, hidden_share)
    tok_rows = tokens.shape[1]
    own_inputs = tokens[0].astype(jnp.float32)
    normed = rms_scaled(own_inputs, attn_gain).astype(jnp.bfloat16)
    length = lengths[0]
    cut_point = tenant_cut[0]
    heads_here = head_block // HEAD_DIM
    flat_qkv = server_qkv.reshape(D, 3 * head_block)
    piece_rows = lax.all_gather(normed, "inner", axis=0, tiled=True)
    row_count = piece_rows.shape[0]
    raw = jnp.dot(piece_rows, flat_qkv, preferred_element_type=jnp.float32).reshape(
        row_count, 3, heads_here, HEAD_DIM
    )
    positions, unused_tenants, unused_places = token_layout(length, cut_point, row_count)
    queries = rotate_heads(raw[:, 0], positions).astype(jnp.bfloat16)
    keys_rot = rotate_heads(raw[:, 1], positions).astype(jnp.bfloat16)
    values_v = raw[:, 2].astype(jnp.bfloat16)
    packed = jnp.stack([queries, keys_rot, values_v], axis=1).reshape(row_count, 3, head_block)
    seq_len = packed.shape[0]
    packed = packed.reshape(seq_len, 3, heads_here, HEAD_DIM)
    queries = packed[:, 0]
    keys_rot = packed[:, 1]
    values_v = packed[:, 2]
    unused_positions, tenants, places = token_layout(length, cut_point, seq_len)
    block_rows = min(seq_len, 512)
    scores = jnp.einsum(
        "qhd,khd->hqk", queries, keys_rot, preferred_element_type=jnp.float32
    ) / math.sqrt(HEAD_DIM)
    allowed = (tenants[0:block_rows, None] == tenants[None, :]) & (
        places[None, :] <= places[0:block_rows, None]
    )
    scores = jnp.where(allowed[None], scores, MASKED)
    weights = jax.nn.softmax(scores, axis=-1).astype(jnp.bfloat16)
    mixed = jnp.einsum("hqk,khd->qhd", weights, values_v, preferred_element_type=jnp.float32)
    block_outputs = mixed.astype(jnp.bfloat16).reshape(block_rows, head_block)
    projected = lax.psum_scatter(
        jnp.dot(block_outputs, out_weight, preferred_element_type=jnp.float32),
        "inner",
        scatter_dimension=0,
        tiled=True,
    )
    residual = own_inputs + projected
    normed_moe = rms_scaled(residual, moe_gain).astype(jnp.bfloat16)
    logits = jnp.dot(normed_moe, router, preferred_element_type=jnp.float32)
    route_ids = expert_ids[0]
    expert_range = jnp.arange(expert_count, dtype=jnp.int32)
    onehot = route_ids[:, :, None] == expert_range[None, None, :]
    chosen = jnp.sum(jnp.where(onehot, logits[:, None, :], 0.0), axis=-1)
    first_weight = jax.nn.sigmoid(chosen[:, 0] - chosen[:, 1])
    capacity = tok_rows * 5 // 16
    flat_hot = onehot.reshape(tok_rows * TOPK, expert_count).astype(jnp.int32)
    ranks = jnp.cumsum(flat_hot, axis=0) - flat_hot
    slot_ids = jnp.sum((expert_range[None, :] * capacity + ranks) * flat_hot, axis=1)
    slot_range = jnp.arange(expert_count * capacity, dtype=jnp.int32)
    dispatch = (slot_ids[None, :] == slot_range[:, None]).astype(jnp.bfloat16)
    repeated = jnp.broadcast_to(normed_moe[:, None, :], (tok_rows, TOPK, D)).reshape(
        tok_rows * TOPK, D
    )
    send_rows = jnp.dot(dispatch, repeated, preferred_element_type=jnp.float32).astype(jnp.bfloat16)
    send_rows = send_rows.reshape(inner_size, local_experts, capacity, D)
    owned = lax.all_to_all(send_rows, "inner", split_axis=0, concat_axis=0, tiled=True)
    arrived = lax.all_gather(owned, "group", axis=0, tiled=True)
    item_count = arrived.shape[0]
    rows_in = arrived[:, 0].reshape(item_count * capacity, D)
    both = jnp.dot(
        rows_in, server_gate_up[0].reshape(D, 2 * hidden_share), preferred_element_type=jnp.float32
    )
    both = both.reshape(item_count * capacity, 2, hidden_share)
    hidden = (jax.nn.silu(both[:, 0]) * both[:, 1]).astype(jnp.bfloat16)
    down_part = jnp.dot(hidden, down_weight[0], preferred_element_type=jnp.float32)
    results = [down_part.reshape(item_count, capacity, D)]
    terms = jnp.stack(results, axis=1).astype(jnp.bfloat16)
    summed = lax.psum_scatter(terms, "group", scatter_dimension=0, tiled=True).astype(jnp.float32)
    expert_out = lax.all_to_all(
        summed.astype(jnp.bfloat16), "inner", split_axis=0, concat_axis=0, tiled=True
    )
    flat_out = expert_out.reshape(expert_count * capacity, D)
    route_slots = slot_ids.reshape(tok_rows, TOPK)
    pick_first = (route_slots[:, 0:1] == slot_range[None, :]).astype(jnp.bfloat16)
    pick_second = (route_slots[:, 1:2] == slot_range[None, :]).astype(jnp.bfloat16)
    first_out = jnp.dot(pick_first, flat_out, preferred_element_type=jnp.float32)
    second_out = jnp.dot(pick_second, flat_out, preferred_element_type=jnp.float32)
    moe = first_weight[:, None] * first_out + (1.0 - first_weight)[:, None] * second_out
    combined = residual + moe
    own_places = lax.axis_index("inner") * tok_rows + jnp.arange(tok_rows, dtype=jnp.int32)
    layer_out = jnp.where((own_places < length)[:, None], combined, 0.0).astype(jnp.bfloat16)
    return (server_qkv, server_gate_up, layer_out[None])


def solution(mesh):
    placed = (
        P("group", "inner", None),
        P("group"),
        P("group"),
        P("group", "inner", None),
        P(("group", "inner"), None, None),
        P(None, ("group", "inner"), None, None),
        P("inner", None),
        P("inner", "group", None),
        P(),
        P(),
        P(),
    )
    return jax.shard_map(
        body,
        mesh=mesh,
        in_specs=placed,
        out_specs=(
            P(None, None, "inner"),
            P("inner", None, None, "group"),
            P("group", "inner", None),
        ),
        check_vma=False,
    )
```

profile of v0, /device:TPU:8, one launch (start us, length us, event | category | flops | bytes accessed | tf_op | source)
XLA Modules:
  0.0 554.5 jit_solution(7805670884036663510)
XLA Ops:
  8.9 12.5 %all_to_all.34 = bf16[18,3,8,256]{3,0,1,2:T(8,128)(2,1)S(1)} all-to-all(bf16[18,3,8,256]{3,0,1,2:T(8,128)(2,1)S(1)} %copy.52), channel_id=1, replica_groups=mesh['group'=16,'inner'=8] {'inner'}, dimensions={2} | all-to-all | bytes 442368 | tf_op jit(solution)/shard_map/all_to_all | solution.py:63
  26.6 50.3 %all-gather.4.cloned.1.call-done = bf16[2304,3,256]{2,0,1:T(8,128)(2,1)} async-done(((bf16[144,3,256]{2,0,1:T(8,128)(2,1)}), bf16[2304,3,256]{2,0,1:T(8,128)(2,1)}) %all-gather.4.cloned.1.call-update) | async-done | bytes 3538960 | tf_op jit(solution)/shard_map/all_gather | solution.py:65
  76.9 5.7 %copy.55 = bf16[2304,3,256]{0,2,1:T(8,128)(2,1)} copy(bf16[2304,3,256]{2,0,1:T(8,128)(2,1)} %all-gather.4.cloned.1.call-done) | data formatting | bytes 7077888 | tf_op jit(solution)/shard_map/all_gather | solution.py:65
  82.6 35.2 %all-gather.6.cloned.1.call-done = bf16[512,2304]{1,0:T(8,128)(2,1)} async-done(((bf16[64,2304]{1,0:T(8,128)(2,1)}), bf16[512,2304]{1,0:T(8,128)(2,1)}) %all-gather.6.cloned.1.call-update) | async-done | bytes 2359312 | tf_op jit(solution)/shard_map/all_gather | solution.py:83
  117.9 4.8 fusion.8
  123.7 4.8 fusion.36
  135.7 55.8 %reduce-scatter.5.cloned.1.call-done = f32[64,2304]{1,0:T(8,128)} async-done(((f32[512,2304]{1,0:T(8,128)}), f32[64,2304]{1,0:T(8,128)}) %reduce-scatter.5.cloned.1.call-update) | async-done | bytes 589840 | tf_op jit(solution)/shard_map/reduce_scatter | solution.py:110
  197.6 18.4 %all_to_all.35 = bf16[8,1,20,2304]{3,2,1,0:T(8,128)(2,1)S(1)} all-to-all(bf16[8,1,20,2304]{3,2,1,0:T(8,128)(2,1)S(1)} %bitcast.90), channel_id=1, replica_groups=mesh['group'=16,'inner'=8] {'inner'}, dimensions={0} | all-to-all | bytes 1474560 | tf_op jit(solution)/shard_map/all_to_all | solution.py:135
  217.3 6.9 %convert_element_type.69 = bf16[8,18,2,5760]{3,2,1,0:T(2,128)(2,1)} convert(f32[8,18,2,5760]{3,2,1,0:T(2,128)} %param.16) | non-fusion elementwise | flops 1658880 | bytes 9953280 | tf_op jit(solution)/shard_map/convert_element_type | solution.py:69
  224.1 11.5 %reshape.215 = bf16[8,1,18,2,16,360]{5,4,3,2,0,1:T(8,128)(2,1)} reshape(bf16[8,18,2,5760]{3,2,1,0:T(2,128)(2,1)} %convert_element_type.69) | data formatting | bytes 6635520 | tf_op jit(solution)/shard_map/reshape | solution.py:69
  235.7 4.7 copy.54
  240.4 61.8 %all_to_all.36 = bf16[128,1,1,18,2,360]{5,4,3,2,1,0:T(2,128)(2,1)} all-to-all(bf16[128,1,1,18,2,360]{5,4,3,2,1,0:T(2,128)(2,1)S(1)} %bitcast.87), channel_id=1, replica_groups=mesh['group'=16,'inner'=8] {'group','inner'}, dimensions={0} | all-to-all | bytes 6635520 | tf_op jit(solution)/shard_map/all_to_all | solution.py:74
  302.2 8.5 %reshape_squeeze_reshape.3 = bf16[2304,720]{1,0:T(8,128)(2,1)} reshape(bf16[128,1,1,18,2,360]{5,4,3,2,1,0:T(2,128)(2,1)} %all_to_all.36) | data formatting | bytes 6635520 | tf_op jit(solution)/shard_map/reshape;squeeze;reshape | solution.py:140
  310.7 5.6 %copy.61 = bf16[720,2304]{1,0:T(8,128)(2,1)} copy(bf16[720,2304]{0,1:T(8,128)(2,1)} %bitcast.88) | data formatting | bytes 6635520 | tf_op jit(solution)/shard_map/dot_general | solution.py:139
  316.3 23.0 %all-gather.8.cloned.1.call-done = bf16[128,1,20,2304]{3,0,2,1:T(8,128)(2,1)} async-done(((bf16[8,1,20,2304]{3,0,2,1:T(8,128)(2,1)}), bf16[128,1,20,2304]{3,0,2,1:T(8,128)(2,1)}) %all-gather.8.cloned.1.call-update) | async-done | bytes 11796496 | tf_op jit(solution)/shard_map/all_gather | solution.py:136
  339.3 14.9 %copy.60 = bf16[128,1,20,2304]{3,2,0,1:T(8,128)(2,1)} copy(bf16[128,1,20,2304]{3,0,2,1:T(8,128)(2,1)} %all-gather.8.cloned.1.call-done) | data formatting | bytes 23592960 | tf_op jit(solution)/shard_map/all_gather | solution.py:136
  354.1 17.2 %reshape.226 = bf16[2560,2304,1]{1,0,2:T(8,128)(2,1)} reshape(bf16[128,1,20,2304]{3,2,0,1:T(8,128)(2,1)} %copy.60) | data formatting | bytes 23592960 | tf_op jit(solution)/shard_map/reshape;squeeze | solution.py:138
  371.3 12.7 %fusion.44 = f32[2560,2,360]{0,2,1:T(8,128)S(1)} fusion(bf16[2560,2304,1]{1,0,2:T(8,128)(2,1)} %reshape.226, bf16[2,360,2304]{2,1,0:T(8,128)(2,1)} %bitcast.91), kind=kOutput, calls=%fused_computation.81 | convolution fusion | flops 8493465600 | bytes 22487040 | tf_op jit(solution)/shard_map/dot_general | solution.py:139
  390.2 4.0 convert_element_type.82
  394.2 8.3 %fusion.37 = bf16[16,8,20,2304]{3,1,0,2:T(8,128)(2,1)S(1)} fusion(bf16[1,360,2304]{2,1,0:T(8,128)(2,1)S(1)} %copy-done, bf16[128,20,360]{2,1,0:T(8,128)(2,1)} %convert_element_type.82), kind=kOutput, calls=%fused_computation.78 | convolution fusion | flops 4252631040 | bytes 15298560 | tf_op jit(solution)/shard_map/dot_general | solution.py:144
  402.5 5.0 copy.72
  407.9 115.4 %reduce-scatter.7.cloned.1.call-done = bf16[8,46080]{1,0:T(8,128)(2,1)} async-done(((bf16[128,46080]{1,0:T(8,128)(2,1)}), bf16[8,46080]{1,0:T(8,128)(2,1)}) %reduce-scatter.7.cloned.1.call-update) | async-done | bytes 737296
  525.5 4.9 all-to-all-start.3
  530.5 10.4 %copy.65 = bf16[1,2304,2,360]{1,3,2,0:T(8,128)(2,1)} copy(bf16[1,2304,2,360]{3,2,1,0:T(2,128)(2,1)} %bitcast.86) | data formatting | bytes 6635520
  (80 shorter events, 36.7 us)
Async XLA Ops:
  7.2 387.0 %copy-start = (bf16[1,360,2304]{2,1,0:T(8,128)(2,1)S(1)}, bf16[1,360,2304]{2,1,0:T(8,128)(2,1)}, u32[]{:S(2)}) copy-start(bf16[1,360,2304]{2,1,0:T(8,128)(2,1)} %param.18) | copy-start | bytes 4976644
  7.2 15.1 %copy-start.2 = (bf16[1,64,2304]{2,1,0:T(8,128)(2,1)S(1)}, bf16[1,64,2304]{2,1,0:T(8,128)(2,1)}, u32[]{:S(2)}) copy-start(bf16[1,64,2304]{2,1,0:T(8,128)(2,1)} %param.11) | copy-start | bytes 884740
  7.2 15.3 %copy-start.11 = (f32[2304]{0:T(1024)S(1)}, f32[2304]{0:T(1024)}, u32[]{:S(2)}) copy-start(f32[2304]{0:T(1024)} %param.19) | copy-start | bytes 27652
  7.2 69.7 %all-gather.4.cloned.1.call-start = ((), (), s32[]{:S(2)}) async-start(), calls=%async_computation.6 | async-start | bytes 3760128 | tf_op jit(solution)/shard_map/all_gather | solution.py:65
  22.2 95.7 %all-gather.6.cloned.1.call-start = ((), (), s32[]{:S(2)}) async-start(), calls=%async_computation.7 | async-start | bytes 2654208 | tf_op jit(solution)/shard_map/all_gather | solution.py:83
  23.3 168.1 %reduce-scatter.5.cloned.1.call-start = ((), (), s32[]{:S(2)}) async-start(), calls=%async_computation.8 | async-start | bytes 5308416 | tf_op jit(solution)/shard_map/reduce_scatter | solution.py:110
  117.9 4.9 copy-start.7
  117.9 4.9 copy-start.8
  128.5 2.8 copy-start.6
  134.3 0.7 copy-start.12
  134.3 58.4 %copy-start.10 = (f32[2304]{0:T(1024)S(1)}, f32[2304]{0:T(1024)}, u32[]{:S(2)}) copy-start(f32[2304]{0:T(1024)} %param.20) | copy-start | bytes 27652
  134.3 204.9 %all-gather.8.cloned.1.call-start = ((), (), s32[]{:S(2)}) async-start(), calls=%async_computation.9 | async-start | bytes 12533760 | tf_op jit(solution)/shard_map/all_gather | solution.py:136
  193.9 0.7 copy-start.4
  217.0 306.3 %reduce-scatter.7.cloned.1.call-start = ((), (), s32[]{:S(2)}) async-start(), calls=%async_computation.10 | async-start | bytes 12533760
  525.5 17.2 %all-to-all-start.3 = ((bf16[8,1,20,2304]{3,2,1,0:T(8,128)(2,1)}), bf16[8,1,20,2304]{3,2,1,0:T(8,128)(2,1)}, u32[]{:S(2)}, u32[]{:S(2)}) async-start(bf16[8,1,20,2304]{3,2,1,0:T(8,128)(2,1)} %copy.64), calls=%async_computation.4 | async-start | bytes 1769472 | tf_op jit(solution)/shard_map/all_to_all | solution.py:148
  530.4 10.4 %copy-start.5 = (bf16[64,2304]{1,0:T(8,128)(2,1)S(1)}, bf16[64,2304]{1,0:T(8,128)(2,1)}, u32[]{:S(2)}) copy-start(bf16[64,2304]{1,0:T(8,128)(2,1)} %copy-done.4) | copy-start | bytes 884740
  530.4 10.4 %copy-start.9 = (bf16[2304,8]{0,1:T(8,128)(2,1)S(1)}, bf16[2304,8]{0,1:T(8,128)(2,1)}, u32[]{:S(2)}) copy-start(bf16[2304,8]{0,1:T(8,128)(2,1)} %param.21) | copy-start | bytes 110596
  530.4 13.9 %copy-start.3 = (f32[64,2304]{1,0:T(8,128)S(1)}, f32[64,2304]{1,0:T(8,128)}, u32[]{:S(2)}) copy-start(f32[64,2304]{1,0:T(8,128)} %reduce-scatter.5.cloned.1.call-done) | copy-start | bytes 1769476
  544.0 2.1 copy-start.1
Sparse Core Ops, SparseCore 0:
  22.3 54.4 all-gather.3
  79.1 38.7 all-gather.5
  134.5 56.9 reduce-scatter.4
  217.2 122.0 all-gather.7
  407.7 115.6 reduce-scatter.6
where the time goes:
time: 558 us; the launch traced here: 554 us
  waiting for transfers between devices  281 us (50%)
  local copies, waits for them, and re-layouts  103 us (18%)
  blocking collectives  92.7 us (17%)
  matrix products  39.1 us (7%)
  other arithmetic  17.4 us (3%)
  between operations  15.4 us (3%)
    unnamed x6, waiting for transfers between devices  116 us
    all_to_all x1, blocking collectives, body(): lax.all_to_all(joined, ('group', 'inner'), split_axis=0, concat_axis=2, t...  61.8 us
    reduce_scatter x1, waiting for transfers between devices, body(): lax.psum_scatter(jnp.dot(block_outputs, out_weight, preferred_element_typ...  55.8 us
    all_gather x1, waiting for transfers between devices, body(): server_qkv = lax.all_gather(head_parts, 'group', axis=0, tiled=True)  50.3 us
    all_gather x1, waiting for transfers between devices, body(): piece_rows = lax.all_gather(normed, 'inner', axis=0, tiled=True)  35.2 us
    all_gather x1, waiting for transfers between devices, body(): arrived = lax.all_gather(owned, 'group', axis=0, tiled=True)  23 us
    unnamed x30, local copies, waits for them, and re-layouts  19.4 us
    all_to_all x1, blocking collectives, body(): lax.all_to_all(send_rows, 'inner', split_axis=0, concat_axis=0, tiled=True)  18.4 us
  transfers between devices with their start and end apart: 6, of which 6 were waited for; matrix products, arithmetic and copies ran while one was open for 10% of the time, Pallas kernels for 0%

commit v1 on v0

v1 whole, which is shorter than its diff:
```python
import math

import jax
import jax.numpy as jnp
from jax import lax
from jax.experimental import pallas as pl
from jax.experimental.pallas import tpu as pltpu
from jax.sharding import PartitionSpec as P

F32 = jnp.float32
BF16 = jnp.bfloat16
MESH = pl.DeviceIdType.MESH
D = 2304
HEAD_DIM = 64
EPS = 1e-05
MASKED = -1e30
ROWS = 18
FFL = 360
FFP = 384
SLOT = 32
CAP = 20
CH = 80
NC = 2
SEQ = 512
TOK = 64


def remote(src, dst, send_sem, recv_sem, device):
    return pltpu.make_async_remote_copy(
        src_ref=src, dst_ref=dst, send_sem=send_sem, recv_sem=recv_sem, device_id=device, device_id_type=MESH
    )


class Spread:
    SENDS = ((0, 0, "R"), (0, 0, "L"), (0, 0, "P"), (0, 1, "R"), (0, 1, "L"), (3, 0, "R"), (1, 1, "L"))
    LANDS = ((3, 0), (1, 0), (0, 1), (3, 1), (1, 1), (2, 0), (2, 1))

    def __init__(self, block, devices, sems, base, relative):
        self.block, self.devices, self.sems, self.base, self.relative = block, devices, sems, base, relative

    def send(self, k):
        dx, dz, way = self.SENDS[k]
        target = self.LANDS[k] if self.relative else (dx, dz)
        n = self.base + k
        return remote(self.block(dx, dz), self.block(*target), self.sems[0].at[n], self.sems[1].at[n], self.devices[way])

    def start(self, *ks):
        for k in ks:
            self.send(k).start()

    def arrived(self, *ks):
        for k in ks:
            n = self.base + k
            land = self.block(*self.LANDS[k])
            remote(land, land, self.sems[0].at[n], self.sems[1].at[n], self.devices[self.SENDS[k][2]]).wait_recv()

    def drain(self):
        for k in range(7):
            self.send(k).wait_send()


class Gather:
    SENDS = ((2, 0, "L"), (2, 1, "R"), (3, 0, "L"), (1, 1, "R"), (3, 1, "L"), (1, 0, "R"), (0, 1, "P"))

    def __init__(self, block, lands, devices, sems, base):
        self.block, self.lands, self.devices, self.sems, self.base = block, lands, devices, sems, base

    def send(self, k):
        dx, dz, way = self.SENDS[k]
        n = self.base + k
        return remote(self.block(dx, dz), self.lands(k), self.sems[0].at[n], self.sems[1].at[n], self.devices[way])

    def start(self, *ks):
        for k in ks:
            self.send(k).start()

    def arrived(self, *ks):
        for k in ks:
            self.send(k).wait_recv()

    def add(self, dx, dz, *ks):
        ref = self.block(dx, dz)
        total = ref[...].astype(F32)
        for k in ks:
            total = total + self.lands(k)[...].astype(F32)
        ref[...] = total.astype(BF16)

    def middle(self):
        self.arrived(0)
        self.add(3, 0, 0)
        self.start(2)
        self.arrived(1)
        self.add(1, 1, 1)
        self.start(3)

    def cross(self):
        self.arrived(3, 4)
        self.add(0, 1, 3, 4)
        self.start(6)

    def total(self):
        self.arrived(2, 5, 6)
        own = self.block(0, 0)[...].astype(F32) + self.lands(6)[...].astype(F32)
        return own + self.lands(2)[...].astype(F32) + self.lands(5)[...].astype(F32)

    def drain(self):
        for k in range(7):
            self.send(k).wait_send()


def where_am_i():
    g = lax.axis_index("group")
    i = lax.axis_index("inner")
    return g, i, g // 4, (g // 2) % 2, g % 2, i // 4, i % 4


def group_id(x, zh, c):
    return x * 4 + zh * 2 + c


def normalize(values, gain):
    mean_square = jnp.mean(values * values, axis=-1, keepdims=True)
    return values * lax.rsqrt(mean_square + EPS) * gain


def front_kernel(
    len_ref, cut_ref, tok_ref, gain_ref, freq_ref, tq_ref, ow_ref, gu_hbm,
    resid_ref, q3_hbm, wt_hbm,
    gu, sbuf, rbuf, qs, qr, w, xb, qkv, att, pb, r1, r2, rz, wt,
    load_sem, gsend, grecv, qsem_s, qsem_r, xsem_s, xsem_r, wsem_s, wsem_r, csem_s, csem_r, psem_s, psem_r, out_sem,
):
    g, i, x, zh, c, zl, y = where_am_i()
    me = g * 8 + i

    def load(k):
        e = lax.rem(i + k, 8)
        return pltpu.make_async_copy(gu_hbm.at[e], gu.at[k], load_sem.at[k])

    for k in range(8):
        load(k).start()

    barrier = pltpu.get_barrier_semaphore()

    def greet(k, carry):
        t = lax.rem(me + k, 128)
        pl.semaphore_signal(barrier, 1, device_id=(t // 8, t % 8), device_id_type=MESH)
        return carry

    lax.fori_loop(1, 128, greet, 0)

    own_inputs = tok_ref[...].astype(F32)
    xb[i] = normalize(own_inputs, gain_ref[...]).astype(BF16)
    for e in range(8):
        cols = slice(e * 256, (e + 1) * 256)
        slab = jnp.concatenate([tq_ref[:, j, cols] for j in range(3)], axis=-1)
        qs[e] = slab.reshape(9, 2, 768).astype(BF16)
    pl.semaphore_wait(barrier, 127)

    inner_devices = {
        "R": (g, zl * 4 + lax.rem(y + 1, 4)),
        "L": (g, zl * 4 + lax.rem(y + 3, 4)),
        "P": (g, (1 - zl) * 4 + y),
    }
    group_devices = {
        "R": (group_id(lax.rem(x + 1, 4), zh, c), i),
        "L": (group_id(lax.rem(x + 3, 4), zh, c), i),
        "P": (group_id(x, 1 - zh, c), i),
    }

    def inner_slot(dx, dz):
        return (zl if dz == 0 else 1 - zl) * 4 + lax.rem(y + dx, 4)

    def group_slot(dx, dz):
        return group_id(lax.rem(x + dx, 4), zh if dz == 0 else 1 - zh, c)

    tokens_all = Spread(lambda dx, dz: xb.at[inner_slot(dx, dz)], inner_devices, (xsem_s, xsem_r), 0, False)
    proj_all = Spread(lambda dx, dz: w.at[:, group_slot(dx, dz)], group_devices, (wsem_s, wsem_r), 0, False)

    def slab_send(k):
        t = lax.rem(i + k, 8)
        return remote(qs.at[t], qr.at[i], qsem_s.at[k], qsem_r.at[k], (g, t))

    for k in range(1, 8):
        slab_send(k).start()
    tokens_all.start(0, 1, 2)
    qr[i] = qs[i]

    def gate_send(tg, e):
        t = tg * 8 + e
        return remote(sbuf.at[t], rbuf.at[me], gsend.at[t], grecv.at[me], (tg, e))

    def ship(k):
        e = lax.rem(i + k, 8)
        load(k).wait()
        for q in range(16):
            sbuf[q * 8 + e] = gu[k, :, :, q * FFL:(q + 1) * FFL].astype(BF16)

        def post(q, carry):
            tg = lax.rem(g + q, 16)
            gate_send(tg, e).start()
            return carry

        if k == 0:
            rbuf[me] = sbuf[me]
            lax.fori_loop(1, 16, post, 0)
        else:
            lax.fori_loop(0, 16, post, 0)

    ship(0)
    ship(1)
    tokens_all.arrived(2)
    tokens_all.start(3, 4)
    for k in range(1, 8):
        s = lax.rem(i + 8 - k, 8)
        remote(qr.at[s], qr.at[s], qsem_s.at[k], qsem_r.at[k], (g, s)).wait_recv()
    block = qr[...].reshape(72, 2, 768).reshape(144, 768)
    for j in range(3):
        w[j, g] = block[:, j * 256:(j + 1) * 256]
    proj_all.start(0, 1, 2)

    other_core = (group_id(x, zh, 1 - c), i)

    def core_send(k, dx, dz):
        s = group_slot(dx, dz)
        return remote(w.at[:, s], w.at[:, s], csem_s.at[k], csem_r.at[k], other_core)

    def core_land(k, dx, dz):
        s = group_id(lax.rem(x + dx, 4), zh if dz == 0 else 1 - zh, 1 - c)
        return remote(w.at[:, s], w.at[:, s], csem_s.at[k], csem_r.at[k], other_core)

    order = ((0, 0), (0, 1), (3, 0), (1, 0), (3, 1), (1, 1), (2, 0), (2, 1))
    core_send(0, 0, 0).start()
    ship(2)
    tokens_all.arrived(0)
    tokens_all.start(5)
    proj_all.arrived(2)
    proj_all.start(3, 4)
    core_send(1, 0, 1).start()
    ship(3)
    tokens_all.arrived(4)
    tokens_all.start(6)
    proj_all.arrived(0)
    proj_all.start(5)
    core_send(2, 3, 0).start()
    proj_all.arrived(1)
    core_send(3, 1, 0).start()
    ship(4)
    proj_all.arrived(4)
    proj_all.start(6)
    core_send(5, 1, 1).start()
    proj_all.arrived(3)
    core_send(4, 3, 1).start()
    ship(5)
    ship(6)
    ship(7)

    length = len_ref[0]
    cut = cut_ref[0]
    places = lax.broadcasted_iota(jnp.int32, (SEQ, 128), 0)
    starts = jnp.where(places >= length, length, jnp.where(places >= cut, cut, 0))
    angles = (places - starts).astype(F32) * freq_ref[...]
    cosine = jnp.cos(angles)
    lane = lax.broadcasted_iota(jnp.int32, (SEQ, 128), 1)
    early = lane % HEAD_DIM < HEAD_DIM // 2
    sine = jnp.sin(angles)
    sine = jnp.where(early, -sine, sine)

    tokens_all.arrived(1, 3, 5, 6)
    proj_all.arrived(5)
    core_send(6, 2, 0).start()
    proj_all.arrived(6)
    core_send(7, 2, 1).start()
    for k, (dx, dz) in enumerate(order):
        core_land(k, dx, dz).wait_recv()
    q3_copy = pltpu.make_async_copy(w, q3_hbm, out_sem.at[0])
    q3_copy.start()

    rows = xb[...].reshape(SEQ, D)
    for j in range(3):
        raw = jnp.dot(rows, w[j].reshape(D, 256), preferred_element_type=F32)
        if j < 2:
            halves = []
            for n in range(2):
                part = raw[:, n * 128:(n + 1) * 128]
                swapped = jnp.where(early, pltpu.roll(part, 96, 1), pltpu.roll(part, 32, 1))
                halves.append(part * cosine + swapped * sine)
            raw = jnp.concatenate(halves, axis=-1)
        qkv[j] = raw.astype(BF16)

    for r in range(4):
        span = (r + 1) * 128
        t = r * 128 + lax.broadcasted_iota(jnp.int32, (128, span), 0)
        s = lax.broadcasted_iota(jnp.int32, (128, span), 1)
        seg_t = jnp.where(t >= length, 2, jnp.where(t >= cut, 1, 0))
        seg_s = jnp.where(s >= length, 2, jnp.where(s >= cut, 1, 0))
        allowed = (s <= t) & (seg_t == seg_s)
        first = lax.broadcasted_iota(jnp.int32, (128, 128), 1) < HEAD_DIM
        for n in range(2):
            cols = slice(n * 128, (n + 1) * 128)
            q = qkv[0, r * 128:(r + 1) * 128, cols]
            k = qkv[1, :span, cols]
            v = qkv[2, :span, cols]
            mixed = []
            for h in range(2):
                keep = first if h == 0 else jnp.logical_not(first)
                qh = jnp.where(keep, q.astype(F32), 0.0).astype(BF16)
                scores = lax.dot_general(qh, k, (((1,), (1,)), ((), ())), preferred_element_type=F32)
                scores = jnp.where(allowed, scores / math.sqrt(HEAD_DIM), MASKED)
                scores = jnp.exp(scores - jnp.max(scores, axis=-1, keepdims=True))
                weights = (scores / jnp.sum(scores, axis=-1, keepdims=True)).astype(BF16)
                mixed.append(jnp.dot(weights, v, preferred_element_type=F32))
            att[r * 128:(r + 1) * 128, cols] = jnp.where(first, mixed[0], mixed[1]).astype(BF16)

    def project(n, carry):
        cols = pl.ds(pl.multiple_of(n * 256, 256), 256)
        part = jnp.dot(att[...], ow_ref[:, cols], preferred_element_type=F32)
        pb[:, :, cols] = part.astype(BF16).reshape(8, TOK, 256)
        return carry

    lax.fori_loop(0, D // 256, project, 0)

    def land(k):
        return r1.at[k] if k < 2 else (rz if k == 6 else r2.at[k - 2])

    back = Gather(lambda dx, dz: pb.at[inner_slot(dx, dz)], land, inner_devices, (psem_s, psem_r), 0)
    back.start(0, 1, 4, 5)

    def settle(k, carry):
        s = lax.rem(me + k, 128)
        remote(rbuf.at[s], rbuf.at[s], gsend.at[s], grecv.at[s], (s // 8, s % 8)).wait_recv()
        return carry

    wt[:, 352:384, :] = jnp.zeros((2, 32, D), BF16)


    back.middle()
    lax.fori_loop(1, 128, settle, 0)
    flat = rbuf.reshape(128 * ROWS, 2, FFL)

    def turn_step(n, carry):
        cols = pl.ds(pl.multiple_of(n * 256, 256), 256)
        wt[:, :FFL, cols] = jnp.transpose(flat[cols], (1, 2, 0))
        return carry

    lax.fori_loop(0, 4, turn_step, 0)
    back.cross()
    lax.fori_loop(4, 9, turn_step, 0)
    wt_copy = pltpu.make_async_copy(wt, wt_hbm, out_sem.at[1])
    wt_copy.start()
    resid_ref[...] = own_inputs + back.total()

    def sent(k, carry):
        t = lax.rem(me + k, 128)
        gate_send(t // 8, t % 8).wait_send()
        return carry

    lax.fori_loop(1, 128, sent, 0)
    for k in range(1, 8):
        slab_send(k).wait_send()
    tokens_all.drain()
    proj_all.drain()
    back.drain()
    for k, (dx, dz) in enumerate(order):
        core_send(k, dx, dz).wait_send()
    q3_copy.wait()
    wt_copy.wait()


def front(tokens, lengths, cuts, gain, freqs, tq, ow, gu):
    vm = pl.BlockSpec(memory_space=pltpu.VMEM)
    sm = pl.BlockSpec(memory_space=pltpu.SMEM)
    hbm = pl.BlockSpec(memory_space=pl.ANY)
    dma = pltpu.SemaphoreType.DMA
    return pl.pallas_call(
        front_kernel,
        name="front",
        out_shape=(
            jax.ShapeDtypeStruct((TOK, D), F32),
            jax.ShapeDtypeStruct((3, 16, 144, 256), BF16),
            jax.ShapeDtypeStruct((2, FFP, D), BF16),
        ),
        in_specs=[sm, sm, vm, vm, vm, vm, vm, hbm],
        out_specs=(vm, hbm, hbm),
        scratch_shapes=[
            pltpu.VMEM((8, ROWS, 2, 5760), F32),
            pltpu.VMEM((128, ROWS, 2, FFL), BF16),
            pltpu.VMEM((128, ROWS, 2, FFL), BF16),
            pltpu.VMEM((8, 9, 2, 768), BF16),
            pltpu.VMEM((8, 9, 2, 768), BF16),
            pltpu.VMEM((3, 16, 144, 256), BF16),
            pltpu.VMEM((8, TOK, D), BF16),
            pltpu.VMEM((3, SEQ, 256), BF16),
            pltpu.VMEM((SEQ, 256), BF16),
            pltpu.VMEM((8, TOK, D), BF16),
            pltpu.VMEM((2, TOK, D), BF16),
            pltpu.VMEM((4, TOK, D), BF16),
            pltpu.VMEM((TOK, D), BF16),
            pltpu.VMEM((2, FFP, D), BF16),
            dma((8,)), dma((128,)), dma((128,)), dma((8,)), dma((8,)), dma((7,)), dma((7,)),
            dma((7,)), dma((7,)), dma((8,)), dma((8,)), dma((7,)), dma((7,)), dma((2,)),
        ],
        compiler_params=pltpu.CompilerParams(collective_id=0, has_side_effects=True, vmem_limit_bytes=50 << 20),
    )(lengths, cuts, tokens, gain, freqs, tq, ow, gu)


def expert_kernel(
    len_ref, resid_ref, gain_ref, rt_ref, ids_ref, pack_ref, wt_ref, dw_ref, out_ref,
    asend, arecv, bsend, brecv, xs, ys, r1, r2, rz, hs, wo, dwo,
    asem_s, asem_r, bsem_s, bsem_r, xsem_s, xsem_r, psem_s, psem_r, csem_s, csem_r,
):
    g, i, x, zh, c, zl, y = where_am_i()
    other_core = (group_id(x, zh, 1 - c), i)
    devices = {
        "R": (group_id(lax.rem(x + 1, 4), zh, c), i),
        "L": (group_id(lax.rem(x + 3, 4), zh, c), i),
        "P": (group_id(x, 1 - zh, c), i),
    }
    barrier = pltpu.get_barrier_semaphore()
    for device in (other_core, devices["R"], devices["L"], devices["P"]):
        pl.semaphore_signal(barrier, 1, device_id=device, device_id_type=MESH)
    for k in range(1, 8):
        pl.semaphore_signal(barrier, 1, device_id=(g, lax.rem(i + k, 8)), device_id_type=MESH)

    residual = resid_ref[...]
    normed = normalize(residual, gain_ref[...]).astype(BF16)
    logits = lax.dot_general(normed, rt_ref[...], (((1,), (1,)), ((), ())), preferred_element_type=F32)
    lanes = lax.broadcasted_iota(jnp.int32, (TOK, 8), 1)
    hot = [(ids_ref[:, n:n + 1] == lanes).astype(F32) for n in range(2)]
    chosen = [jnp.sum(h * logits, axis=-1, keepdims=True) for h in hot]
    first_weight = jax.nn.sigmoid(chosen[0] - chosen[1])
    before = lax.broadcasted_iota(jnp.int32, (TOK, TOK), 1) < lax.broadcasted_iota(jnp.int32, (TOK, TOK), 0)
    ranks = jnp.dot(before.astype(BF16), (hot[0] + hot[1]).astype(BF16), preferred_element_type=F32)
    base = (lanes * SLOT).astype(F32)
    slots = lax.broadcasted_iota(jnp.int32, (TOK, 8 * SLOT), 1).astype(F32)
    pick = [(jnp.sum(h * (base + ranks), axis=-1, keepdims=True) == slots).astype(F32) for h in hot]
    rows = lax.dot_general(
        (pick[0] + pick[1]).astype(BF16), normed, (((0,), (0,)), ((), ())), preferred_element_type=F32
    )
    asend[...] = rows.astype(BF16).reshape(8, SLOT, D)
    pl.semaphore_wait(barrier, 11)

    def out_send(k):
        t = lax.rem(i + k, 8)
        return remote(asend.at[t], arecv.at[k], asem_s.at[k], asem_r.at[k], (g, t))

    for k in range(1, 8):
        out_send(k).start()
    arecv[0] = asend[i]
    core_copies = [
        remote(wt_ref, wo, csem_s.at[0], csem_r.at[0], other_core),
        remote(dw_ref, dwo, csem_s.at[1], csem_r.at[1], other_core),
    ]
    for copy in core_copies:
        copy.start()

    place = {(0, 0): (0, 0), (0, 1): (0, 1), (2, 0): (1, 0), (2, 1): (1, 1), (1, 0): (2, 0), (1, 1): (2, 1),
             (3, 0): (3, 0), (3, 1): (3, 1)}

    def make(cc):
        def block(ref):
            return lambda dx, dz: ref.at[(cc,) + place[(dx, dz)]]

        def land(k):
            return r1.at[cc, k] if k < 2 else (rz.at[cc] if k == 6 else r2.at[cc, k - 2])

        spread = Spread(block(xs), devices, (xsem_s, xsem_r), 7 * cc, True)
        gather = Gather(block(ys), land, devices, (psem_s, psem_r), 7 * cc)
        return spread, gather

    spreads, gathers = zip(*[make(cc) for cc in range(NC)])

    def pack(cc):
        rows_in = arecv[4 * cc:4 * cc + 4].reshape(4 * SLOT, D)
        packed = lax.dot_general(
            pack_ref[...], rows_in, (((1,), (0,)), ((), ())), preferred_element_type=F32
        )
        xs[cc, 0, 0] = packed.astype(BF16)

    for cc in range(NC):
        for k in range(4 * cc, 4 * cc + 4):
            if k:
                out_send(k).wait_recv()
        pack(cc)
        spreads[cc].start(0, 1, 2)

    def feed(cc, start, count):
        m = count * 2 * CH

        def up(t, carry):
            r = pl.ds(pl.multiple_of(t * 128, 128), 128)
            rows_in = xs[cc, start:start + count].reshape(m, D)
            for n, ref in enumerate((wt_ref, wo)):
                both = jnp.concatenate([ref[0, r, :], ref[1, r, :]], axis=0)
                parts = lax.dot_general(rows_in, both, (((1,), (1,)), ((), ())), preferred_element_type=F32)
                hidden = jax.nn.silu(parts[:, :128]) * parts[:, 128:]
                hs[:m, pl.ds(pl.multiple_of(n * FFP + t * 128, 128), 128)] = hidden.astype(BF16)
            return carry

        lax.fori_loop(0, 3, up, 0)

        def down(n, carry):
            cols = pl.ds(pl.multiple_of(n * 256, 256), 256)
            part = jnp.dot(hs[:m, :FFP], dw_ref[:, cols], preferred_element_type=F32)
            part = part + jnp.dot(hs[:m, FFP:], dwo[:, cols], preferred_element_type=F32)
            ys[cc, start:start + count, :, :, cols] = part.astype(BF16).reshape(count, 2, CH, 256)
            return carry

        lax.fori_loop(0, D // 256, down, 0)

    def back_send(k):
        s = lax.rem(i + 8 - k, 8)
        return remote(bsend.at[k], brecv.at[i], bsem_s.at[k], bsem_r.at[k], (g, s))

    def finish(cc):
        total = gathers[cc].total().astype(BF16)
        spaced = lax.dot_general(
            pack_ref[...], total, (((0,), (0,)), ((), ())), preferred_element_type=F32
        ).astype(BF16).reshape(4, SLOT, D)
        bsend[4 * cc:4 * cc + 4] = spaced
        for k in range(4 * cc, 4 * cc + 4):
            if k:
                back_send(k).start()
            else:
                brecv[i] = bsend[0]

    for cc in range(NC):
        spreads[cc].arrived(2)
        spreads[cc].start(3, 4)
    spreads[0].arrived(0)
    spreads[0].start(5)
    for copy in core_copies:
        copy.wait_recv()
    feed(0, 0, 1)
    spreads[0].arrived(4)
    spreads[0].start(6)
    spreads[1].arrived(0)
    spreads[1].start(5)
    spreads[0].arrived(1, 3)
    feed(0, 2, 2)
    gathers[0].start(4, 5)
    spreads[1].arrived(4)
    spreads[1].start(6)
    spreads[0].arrived(5, 6)
    feed(0, 1, 1)
    gathers[0].start(0, 1)
    feed(1, 0, 1)
    spreads[1].arrived(1, 3)
    gathers[0].middle()
    feed(1, 2, 2)
    gathers[1].start(4, 5)
    spreads[1].arrived(5, 6)
    feed(1, 1, 1)
    gathers[1].start(0, 1)
    gathers[0].cross()
    gathers[1].middle()
    finish(0)
    gathers[1].cross()
    finish(1)

    own_places = i * TOK + lax.broadcasted_iota(jnp.int32, (TOK, 1), 0)
    live = own_places < len_ref[0]
    for k in range(1, 8):
        e = lax.rem(i + k, 8)
        remote(brecv.at[e], brecv.at[e], bsem_s.at[k], bsem_r.at[k], (g, e)).wait_recv()
    flat = brecv[...].reshape(8 * SLOT, D)
    first_out = jnp.dot(pick[0].astype(BF16), flat, preferred_element_type=F32)
    second_out = jnp.dot(pick[1].astype(BF16), flat, preferred_element_type=F32)
    combined = residual + (first_weight * first_out + (1.0 - first_weight) * second_out)
    out_ref[...] = jnp.where(live, combined, 0.0).astype(BF16)

    for k in range(1, 8):
        out_send(k).wait_send()
        back_send(k).wait_send()
    for copy in core_copies:
        copy.wait_send()
    for cc in range(NC):
        spreads[cc].drain()
        gathers[cc].drain()


def experts(lengths, resid, gain, rt, ids, pack, wt, dw):
    vm = pl.BlockSpec(memory_space=pltpu.VMEM)
    sm = pl.BlockSpec(memory_space=pltpu.SMEM)
    dma = pltpu.SemaphoreType.DMA
    return pl.pallas_call(
        expert_kernel,
        name="experts",
        out_shape=jax.ShapeDtypeStruct((TOK, D), BF16),
        in_specs=[sm, vm, vm, vm, vm, vm, vm, vm],
        out_specs=vm,
        scratch_shapes=[
            pltpu.VMEM((8, SLOT, D), BF16),
            pltpu.VMEM((8, SLOT, D), BF16),
            pltpu.VMEM((8, SLOT, D), BF16),
            pltpu.VMEM((8, SLOT, D), BF16),
            pltpu.VMEM((NC, 4, 2, CH, D), BF16),
            pltpu.VMEM((NC, 4, 2, CH, D), BF16),
            pltpu.VMEM((NC, 2, CH, D), BF16),
            pltpu.VMEM((NC, 4, CH, D), BF16),
            pltpu.VMEM((NC, CH, D), BF16),
            pltpu.VMEM((4 * CH, 2 * FFP), BF16),
            pltpu.VMEM((2, FFP, D), BF16),
            pltpu.VMEM((FFP, D), BF16),
            dma((8,)), dma((8,)), dma((8,)), dma((8,)), dma((7 * NC,)), dma((7 * NC,)),
            dma((7 * NC,)), dma((7 * NC,)), dma((2,)), dma((2,)),
        ],
        compiler_params=pltpu.CompilerParams(collective_id=1, has_side_effects=True, vmem_limit_bytes=50 << 20),
    )(lengths, resid, gain, rt, ids, pack, wt, dw)


def body(
    tokens,
    lengths,
    tenant_cut,
    expert_ids,
    trainer_qkv,
    trainer_gate_up,
    out_weight,
    down_weight,
    attn_gain,
    moe_gain,
    router,
):
    half = HEAD_DIM // 2
    freqs = jnp.exp(-math.log(10000.0) * jnp.arange(half, dtype=F32) / half)
    freqs = jnp.tile(freqs, 4)[None, :]
    resid, q3, wt = front(
        tokens[0], lengths, tenant_cut, attn_gain[None, :], freqs, trainer_qkv, out_weight, trainer_gate_up
    )
    server_qkv = jnp.transpose(q3.reshape(3, D, 256), (1, 0, 2))
    server_gate_up = jnp.transpose(wt[:, :FFL, :], (2, 0, 1))[None]
    dw = jnp.pad(down_weight[0], ((0, FFP - FFL), (0, 0)))
    packed = jnp.arange(CH, dtype=jnp.int32)
    spaced = (packed // CAP) * SLOT + packed % CAP
    pack = (spaced[:, None] == jnp.arange(4 * SLOT, dtype=jnp.int32)[None, :]).astype(BF16)
    layer_out = experts(lengths, resid, moe_gain[None, :], router.T, expert_ids[0], pack, wt, dw)
    return (server_qkv, server_gate_up, layer_out[None])


def solution(mesh):
    placed = (
        P("group", "inner", None),
        P("group"),
        P("group"),
        P("group", "inner", None),
        P(("group", "inner"), None, None),
        P(None, ("group", "inner"), None, None),
        P("inner", None),
        P("inner", "group", None),
        P(),
        P(),
        P(),
    )
    return jax.shard_map(
        body,
        mesh=mesh,
        in_specs=placed,
        out_specs=(
            P(None, None, "inner"),
            P("inner", None, None, "group"),
            P("group", "inner", None),
        ),
        check_vma=False,
    )
```

time: 558 us -> 276 us (0.49)
  waiting for transfers between devices: 281 us -> 0 us
  Pallas kernels: 0 us -> 263 us
  blocking collectives: 92.7 us -> 0 us
  local copies, waits for them, and re-layouts: 103 us -> 10.4 us
  matrix products: 39.1 us -> 0 us
  other arithmetic: 17.4 us -> 0.1 us
  between operations: 15.4 us -> 2.04 us
    pallas_call x0 -> x2, Pallas kernels: none -> 263 us  [the longest x1 150 us: experts(): pl.pallas_call(expert_kernel, name='experts', out_shape=jax.ShapeDtypeStr...]
    unnamed x6 -> x0, waiting for transfers between devices: 116 us -> none
    all_gather x3 -> x0, waiting for transfers between devices: 109 us -> none  [the longest x1 50.3 us: body(): server_qkv = lax.all_gather(head_parts, 'group', axis=0, tiled=True)]
    all_to_all x3 -> x0, blocking collectives: 92.7 us -> none  [the longest x1 61.8 us: body(): lax.all_to_all(joined, ('group', 'inner'), split_axis=0, concat_axis=2, t...]
    reduce_scatter x1 -> x0, waiting for transfers between devices: 55.8 us -> none  [body(): lax.psum_scatter(jnp.dot(block_outputs, out_weight, preferred_element_typ...]
    dot_general x9 -> x0, matrix products: 34.2 us -> none  [the longest x1 12.7 us: body(): jnp.dot(rows_in, server_gate_up[0].reshape(D, 2 * hidden_share), preferre...]
    another operation x2, local copies, waits for them, and re-layouts: 25.7 us -> 0.09 us  [body(): freqs = jnp.tile(freqs, 4)[None, :]]
    all_gather x2 -> x0, local copies, waits for them, and re-layouts: 20.6 us -> none  [the longest x1 14.9 us: body(): arrived = lax.all_gather(owned, 'group', axis=0, tiled=True)]
  transfers between devices with their start and end apart: 6 -> 0, of which waited for: 6 -> 0; matrix products, arithmetic and copies ran while one was open for 10% -> 0% of each run, Pallas kernels for 0% -> 0%
where the time goes in v1:
time: 276 us
  Pallas kernels  263 us (95%)
  local copies, waits for them, and re-layouts  10.4 us (4%)
    pallas_call x1, Pallas kernels, experts(): pl.pallas_call(expert_kernel, name='experts', out_shape=jax.ShapeDtypeStr...  150 us
    pallas_call x1, Pallas kernels, front(): pl.pallas_call(front_kernel, name='front', out_shape=(jax.ShapeDtypeStruc...  113 us
    unnamed x20, local copies, waits for them, and re-layouts  7.45 us

profile of v1, /device:TPU:8, one launch (start us, length us, event | category | flops | bytes accessed | tf_op | source)
XLA Modules:
  0.0 276.0 jit_solution(12498335896223074689)
XLA Ops:
  1.3 0.7 broadcast_in_dim.14.gain_ref
  2.0 0.1 broadcast_in_dim_tile.3.freq_ref
  2.8 0.0 copy-start
  2.8 1.3 copy-done
  4.0 0.0 copy-start.1
  4.0 1.1 copy-done.1
  5.1 0.0 copy-start.2
  5.1 1.0 copy-done.2
  6.1 113.4 %front.1 = (f32[64,2304]{1,0:T(8,128)S(1)}, bf16[3,16,144,256]{3,2,1,0:T(8,128)(2,1)}, bf16[2,384,2304]{2,1,0:T(8,128)(2,1)}) custom-call(s32[1]{0:T(128)S(6)} %copy.17.len_ref, s32[1]{0:T(128)S(6)} %copy.18.cut_ref, bf16[64,2304]{1,0:T(8,128)(2,1)S(1)} %bitcast.13, f32[1,2304]{1,0:T(1,128)S(1)} %broadcast_in_dim.14.gain_ref, ...), custom_call_target="tpu_custom_call" | custom-call | tf_op jit(solution)/shard_map/front/pallas_call | solution.py:374
  119.5 0.0 copy-start.3
  119.5 0.0 copy-done.6
  119.5 0.1 pad.4.dw_ref
  119.7 0.0 copy-done.8
  119.7 0.1 copy.14.ids_ref
  119.8 0.1 fusion.pack_ref
  119.9 0.0 copy-done.7
  119.9 0.4 copy-done.3
  120.3 150.0 %experts.1 = bf16[64,2304]{1,0:T(8,128)(2,1)S(1)} custom-call(s32[1]{0:T(128)S(6)} %copy.17.len_ref, f32[64,2304]{1,0:T(8,128)S(1)} %get-tuple-element.8.resid_ref, f32[1,2304]{1,0:T(1,128)S(1)} %broadcast_in_dim.16.gain_ref, bf16[8,2304]{1,0:T(8,128)(2,1)S(1)} %bitcast.14, s32[64,2]{1,0:T(8,128)S(1)} %copy.14.ids_ref, bf16[80,128]{1,0:T(8,128)(2,1)S(1)} %fusion.pack_ref, ...), custom_call_target="tpu_custom_call" | custom-call | tf_op jit(solution)/shard_map/experts/pallas_call | solution.py:585
  270.3 0.0 copy-start.5
  270.3 0.0 copy-done.4
  270.3 1.9 slice_bitcast_fusion
  272.3 1.2 copy-done.5
  273.5 1.8 copy.19
  275.3 0.7 copy.20
  (8 shorter events, 0.0 us)
Async XLA Ops:
  2.8 1.3 copy-start
  4.0 1.1 copy-start.1
  5.1 1.0 copy-start.2
  6.1 113.5 %copy-start.6 = (bf16[1,360,2304]{2,1,0:T(8,128)(2,1)S(1)}, bf16[1,360,2304]{2,1,0:T(8,128)(2,1)}, u32[]{:S(2)}) copy-start(bf16[1,360,2304]{2,1,0:T(8,128)(2,1)} %param.18) | copy-start | bytes 4976644
  6.1 113.6 %copy-start.8 = (s32[1,64,2]{1,2,0:T(2,128)S(1)}, s32[1,64,2]{1,2,0:T(2,128)}, u32[]{:S(2)}) copy-start(s32[1,64,2]{1,2,0:T(2,128)} %param.14) | copy-start | bytes 1540
  6.1 113.8 %copy-start.7 = (f32[2304]{0:T(1024)S(1)}, f32[2304]{0:T(1024)}, u32[]{:S(2)}) copy-start(f32[2304]{0:T(1024)} %param.20) | copy-start | bytes 27652
  119.5 0.8 copy-start.3
  119.8 150.6 %copy-start.4 = (bf16[2,384,2304]{2,1,0:T(8,128)(2,1)S(1)}, bf16[2,384,2304]{2,1,0:T(8,128)(2,1)}, u32[]{:S(2)}) copy-start(bf16[2,384,2304]{2,1,0:T(8,128)(2,1)} %get-tuple-element.7.wt_ref) | copy-start | bytes 10616836
  270.3 3.2 %copy-start.5 = (bf16[3,16,144,256]{3,2,1,0:T(8,128)(2,1)S(1)}, bf16[3,16,144,256]{3,2,1,0:T(8,128)(2,1)}, u32[]{:S(2)}) copy-start(bf16[3,16,144,256]{3,2,1,0:T(8,128)(2,1)} %get-tuple-element.6) | copy-start | bytes 10616836

commit v2 on v1

v2 whole, which is shorter than its diff:
```python
import math

import jax
import jax.numpy as jnp
from jax import lax
from jax.experimental import pallas as pl
from jax.experimental.pallas import tpu as pltpu
from jax.sharding import PartitionSpec as P

F32 = jnp.float32
BF16 = jnp.bfloat16
MESH = pl.DeviceIdType.MESH
D = 2304
HEAD_DIM = 64
EPS = 1e-05
MASKED = -1e30
ROWS = 18
FFL = 360
FFP = 384
CAP = 20
CH = 80
NC = 2
SEQ = 512
TOK = 64


def remote(src, dst, send_sem, recv_sem, device):
    return pltpu.make_async_remote_copy(
        src_ref=src, dst_ref=dst, send_sem=send_sem, recv_sem=recv_sem, device_id=device, device_id_type=MESH
    )


class Spread:
    SENDS = ((0, 0, "R"), (0, 0, "L"), (0, 0, "P"), (0, 1, "R"), (0, 1, "L"), (3, 0, "R"), (1, 1, "L"))
    LANDS = ((3, 0), (1, 0), (0, 1), (3, 1), (1, 1), (2, 0), (2, 1))

    def __init__(self, block, devices, sems, base, relative):
        self.block, self.devices, self.sems, self.base, self.relative = block, devices, sems, base, relative

    def send(self, k):
        dx, dz, way = self.SENDS[k]
        target = self.LANDS[k] if self.relative else (dx, dz)
        n = self.base + k
        return remote(self.block(dx, dz), self.block(*target), self.sems[0].at[n], self.sems[1].at[n], self.devices[way])

    def start(self, *ks):
        for k in ks:
            self.send(k).start()

    def arrived(self, *ks):
        for k in ks:
            n = self.base + k
            land = self.block(*self.LANDS[k])
            remote(land, land, self.sems[0].at[n], self.sems[1].at[n], self.devices[self.SENDS[k][2]]).wait_recv()

    def drain(self):
        for k in range(7):
            self.send(k).wait_send()


class Gather:
    SENDS = ((2, 0, "L"), (2, 1, "R"), (3, 0, "L"), (1, 1, "R"), (3, 1, "L"), (1, 0, "R"), (0, 1, "P"))

    def __init__(self, block, lands, devices, sems, base):
        self.block, self.lands, self.devices, self.sems, self.base = block, lands, devices, sems, base

    def send(self, k):
        dx, dz, way = self.SENDS[k]
        n = self.base + k
        return remote(self.block(dx, dz), self.lands(k), self.sems[0].at[n], self.sems[1].at[n], self.devices[way])

    def start(self, *ks):
        for k in ks:
            self.send(k).start()

    def arrived(self, *ks):
        for k in ks:
            self.send(k).wait_recv()

    def add(self, dx, dz, *ks):
        ref = self.block(dx, dz)
        total = ref[...].astype(F32)
        for k in ks:
            total = total + self.lands(k)[...].astype(F32)
        ref[...] = total.astype(BF16)

    def middle(self):
        self.arrived(0)
        self.add(3, 0, 0)
        self.start(2)
        self.arrived(1)
        self.add(1, 1, 1)
        self.start(3)

    def cross(self):
        self.arrived(3, 4)
        self.add(0, 1, 3, 4)
        self.start(6)

    def total(self):
        self.arrived(2, 5, 6)
        own = self.block(0, 0)[...].astype(F32) + self.lands(6)[...].astype(F32)
        return own + self.lands(2)[...].astype(F32) + self.lands(5)[...].astype(F32)

    def drain(self):
        for k in range(7):
            self.send(k).wait_send()


class RoutedSpread:
    ALL, TOP, LOW = (0, CH), (0, 48), (48, CH)
    STEPS = (
        ((0, 0), ALL, "R", (3, 0)),
        ((0, 0), ALL, "L", (1, 0)),
        ((0, 0), ALL, "P", (0, 1)),
        ((0, 1), ALL, "R", (3, 1)),
        ((0, 1), ALL, "L", (1, 1)),
        ((3, 0), TOP, "R", (2, 0)),
        ((1, 0), LOW, "L", (2, 0)),
        ((2, 0), TOP, "P", (2, 1)),
        ((2, 0), LOW, "P", (2, 1)),
    )

    def __init__(self, block, devices, sems, base):
        self.block, self.devices, self.sems, self.base = block, devices, sems, base

    def send(self, k):
        source, (lo, hi), way, target = self.STEPS[k]
        n = self.base + k
        return remote(
            self.block(*source).at[lo:hi], self.block(*target).at[lo:hi],
            self.sems[0].at[n], self.sems[1].at[n], self.devices[way],
        )

    def start(self, *ks):
        for k in ks:
            self.send(k).start()

    def arrived(self, *ks):
        for k in ks:
            self.send(k).wait_recv()

    def drain(self):
        for k in range(9):
            self.send(k).wait_send()


class RoutedGather:
    ALL, TOP, LOW = (0, CH), (0, 48), (48, CH)
    STEPS = (
        ((2, 1), ALL, "P", 0),
        ((2, 0), TOP, "L", 1),
        ((2, 0), LOW, "R", 1),
        ((3, 0), ALL, "L", 2),
        ((1, 0), ALL, "R", 3),
        ((3, 1), ALL, "L", 4),
        ((1, 1), ALL, "R", 5),
        ((0, 1), ALL, "P", 6),
    )

    def __init__(self, block, lands, devices, sems, base):
        self.block, self.lands, self.devices, self.sems, self.base = block, lands, devices, sems, base

    def send(self, k):
        source, (lo, hi), way, land = self.STEPS[k]
        n = self.base + k
        return remote(
            self.block(*source).at[lo:hi], self.lands(land).at[lo:hi],
            self.sems[0].at[n], self.sems[1].at[n], self.devices[way],
        )

    def start(self, *ks):
        for k in ks:
            self.send(k).start()

    def arrived(self, *ks):
        for k in ks:
            self.send(k).wait_recv()

    def add(self, place, span, *lands):
        lo, hi = span
        ref = self.block(*place).at[lo:hi]
        total = ref[...].astype(F32)
        for n in lands:
            total = total + self.lands(n).at[lo:hi][...].astype(F32)
        ref[...] = total.astype(BF16)

    def far(self):
        self.arrived(0)
        self.add((2, 0), self.TOP, 0)
        self.start(1)
        self.add((2, 0), self.LOW, 0)
        self.start(2)

    def middle(self):
        self.arrived(1)
        self.add((3, 0), self.TOP, 1)
        self.start(3)
        self.arrived(2)
        self.add((1, 0), self.LOW, 1)
        self.start(4)

    def cross(self):
        self.arrived(5, 6)
        self.add((0, 1), self.ALL, 4, 5)
        self.start(7)

    def total(self):
        self.arrived(3, 4, 7)
        total = self.block(0, 0)[...].astype(F32)
        for n in (2, 3, 6):
            total = total + self.lands(n)[...].astype(F32)
        return total

    def drain(self):
        for k in range(8):
            self.send(k).wait_send()


def where_am_i():
    g = lax.axis_index("group")
    i = lax.axis_index("inner")
    return g, i, g // 4, (g // 2) % 2, g % 2, i // 4, i % 4


def group_id(x, zh, c):
    return x * 4 + zh * 2 + c


def normalize(values, gain):
    mean_square = jnp.mean(values * values, axis=-1, keepdims=True)
    return values * lax.rsqrt(mean_square + EPS) * gain


def layer_kernel(
    len_ref, cut_ref, gain_ref, freq_ref, mgain_ref, rt_ref, ids_ref, tok_hbm, tq_hbm, ow_hbm, dw_hbm, gu_hbm,
    out_ref, q3_hbm, wt_hbm,
    tok_ref, tq_ref, ow_ref, dw_ref, resid_ref,
    gu, sbuf, rbuf, qs, qr, w, xb, qkv, att, pb, r1, r2, rz, wt,
    asend, arecv, bsend, brecv, xs, ys, lands, hs, wo, dwo,
    in_sem, load_sem, gsend, grecv, qsem_s, qsem_r, xsem_s, xsem_r, wsem_s, wsem_r, csem_s, csem_r, psem_s, psem_r,
    out_sem, asem_s, asem_r, bsem_s, bsem_r, ysem_s, ysem_r, dsem_s, dsem_r, esem_s, esem_r,
):
    g, i, x, zh, c, zl, y = where_am_i()
    me = g * 8 + i

    def load(k):
        e = lax.rem(i + k, 8)
        return pltpu.make_async_copy(gu_hbm.at[e], gu.at[k % 2], load_sem.at[k])

    parts_in = [
        pltpu.make_async_copy(tq_hbm, tq_ref, in_sem.at[0]),
        pltpu.make_async_copy(tok_hbm, tok_ref, in_sem.at[1]),
        pltpu.make_async_copy(ow_hbm, ow_ref, in_sem.at[2]),
        pltpu.make_async_copy(dw_hbm, dw_ref.at[:FFL], in_sem.at[3]),
    ]
    parts_in[1].start()
    parts_in[0].start()
    load(0).start()
    load(1).start()
    parts_in[2].start()
    parts_in[3].start()

    barrier = pltpu.get_barrier_semaphore()

    def greet(k, carry):
        t = lax.rem(me + k, 128)
        pl.semaphore_signal(barrier, 1, device_id=(t // 8, t % 8), device_id_type=MESH)
        return carry

    lax.fori_loop(1, 128, greet, 0)

    parts_in[1].wait()
    own_inputs = tok_ref[...].astype(F32)
    xb[i] = normalize(own_inputs, gain_ref[...]).astype(BF16)
    parts_in[0].wait()
    for e in range(8):
        cols = slice(e * 256, (e + 1) * 256)
        slab = jnp.concatenate([tq_ref[:, j, cols] for j in range(3)], axis=-1)
        qs[e] = slab.reshape(9, 2, 768).astype(BF16)
    pl.semaphore_wait(barrier, 127)

    inner_devices = {
        "R": (g, zl * 4 + lax.rem(y + 1, 4)),
        "L": (g, zl * 4 + lax.rem(y + 3, 4)),
        "P": (g, (1 - zl) * 4 + y),
    }
    group_devices = {
        "R": (group_id(lax.rem(x + 1, 4), zh, c), i),
        "L": (group_id(lax.rem(x + 3, 4), zh, c), i),
        "P": (group_id(x, 1 - zh, c), i),
    }

    def inner_slot(dx, dz):
        return (zl if dz == 0 else 1 - zl) * 4 + lax.rem(y + dx, 4)

    def group_slot(dx, dz):
        return group_id(lax.rem(x + dx, 4), zh if dz == 0 else 1 - zh, c)

    tokens_all = Spread(lambda dx, dz: xb.at[inner_slot(dx, dz)], inner_devices, (xsem_s, xsem_r), 0, False)
    proj_all = Spread(lambda dx, dz: w.at[:, group_slot(dx, dz)], group_devices, (wsem_s, wsem_r), 0, False)

    def slab_send(k):
        t = lax.rem(i + k, 8)
        return remote(qs.at[t], qr.at[i], qsem_s.at[k], qsem_r.at[k], (g, t))

    for k in range(1, 8):
        slab_send(k).start()
    tokens_all.start(0, 1, 2)
    qr[i] = qs[i]

    def gate_send(tg, e):
        t = tg * 8 + e
        return remote(sbuf.at[t], rbuf.at[me], gsend.at[t], grecv.at[me], (tg, e))

    def ship(k):
        e = lax.rem(i + k, 8)
        load(k).wait()
        for q in range(16):
            sbuf[q * 8 + e] = gu[k % 2, :, :, q * FFL:(q + 1) * FFL].astype(BF16)
        if k < 6:
            load(k + 2).start()

        def post(q, carry):
            tg = lax.rem(g + q, 16)
            gate_send(tg, e).start()
            return carry

        if k == 0:
            rbuf[me] = sbuf[me]
            lax.fori_loop(1, 16, post, 0)
        else:
            lax.fori_loop(0, 16, post, 0)

    ship(0)
    ship(1)
    tokens_all.arrived(2)
    tokens_all.start(3, 4)
    for k in range(1, 8):
        s = lax.rem(i + 8 - k, 8)
        remote(qr.at[s], qr.at[s], qsem_s.at[k], qsem_r.at[k], (g, s)).wait_recv()
    block = qr[...].reshape(72, 2, 768).reshape(144, 768)
    for j in range(3):
        w[j, g] = block[:, j * 256:(j + 1) * 256]
    proj_all.start(0, 1, 2)

    other_core = (group_id(x, zh, 1 - c), i)

    def core_send(k, dx, dz):
        s = group_slot(dx, dz)
        return remote(w.at[:, s], w.at[:, s], csem_s.at[k], csem_r.at[k], other_core)

    def core_land(k, dx, dz):
        s = group_id(lax.rem(x + dx, 4), zh if dz == 0 else 1 - zh, 1 - c)
        return remote(w.at[:, s], w.at[:, s], csem_s.at[k], csem_r.at[k], other_core)

    order = ((0, 0), (0, 1), (3, 0), (1, 0), (3, 1), (1, 1), (2, 0), (2, 1))
    core_send(0, 0, 0).start()
    ship(2)
    tokens_all.arrived(0)
    tokens_all.start(5)
    proj_all.arrived(2)
    proj_all.start(3, 4)
    core_send(1, 0, 1).start()
    ship(3)
    tokens_all.arrived(4)
    tokens_all.start(6)
    proj_all.arrived(0)
    proj_all.start(5)
    core_send(2, 3, 0).start()
    proj_all.arrived(1)
    core_send(3, 1, 0).start()
    ship(4)
    proj_all.arrived(4)
    proj_all.start(6)
    core_send(5, 1, 1).start()
    proj_all.arrived(3)
    core_send(4, 3, 1).start()
    ship(5)

    length = len_ref[0]
    cut = cut_ref[0]
    places = lax.broadcasted_iota(jnp.int32, (SEQ, 128), 0)
    starts = jnp.where(places >= length, length, jnp.where(places >= cut, cut, 0))
    angles = (places - starts).astype(F32) * freq_ref[...]
    cosine = jnp.cos(angles)
    lane = lax.broadcasted_iota(jnp.int32, (SEQ, 128), 1)
    early = lane % HEAD_DIM < HEAD_DIM // 2
    sine = jnp.sin(angles)
    sine = jnp.where(early, -sine, sine)

    tokens_all.arrived(1, 3, 5, 6)
    proj_all.arrived(5)
    core_send(6, 2, 0).start()
    proj_all.arrived(6)
    core_send(7, 2, 1).start()
    for k, (dx, dz) in enumerate(order):
        core_land(k, dx, dz).wait_recv()
    q3_copy = pltpu.make_async_copy(w, q3_hbm, out_sem.at[0])
    q3_copy.start()

    rows = xb[...].reshape(SEQ, D)
    for j in range(3):
        raw = jnp.dot(rows, w[j].reshape(D, 256), preferred_element_type=F32)
        if j < 2:
            halves = []
            for n in range(2):
                part = raw[:, n * 128:(n + 1) * 128]
                swapped = jnp.where(early, pltpu.roll(part, 96, 1), pltpu.roll(part, 32, 1))
                halves.append(part * cosine + swapped * sine)
            raw = jnp.concatenate(halves, axis=-1)
        qkv[j] = raw.astype(BF16)

    ship(6)
    for r in range(4):
        span = (r + 1) * 128
        t = r * 128 + lax.broadcasted_iota(jnp.int32, (128, span), 0)
        s = lax.broadcasted_iota(jnp.int32, (128, span), 1)
        seg_t = jnp.where(t >= length, 2, jnp.where(t >= cut, 1, 0))
        seg_s = jnp.where(s >= length, 2, jnp.where(s >= cut, 1, 0))
        allowed = (s <= t) & (seg_t == seg_s)
        first = lax.broadcasted_iota(jnp.int32, (128, 128), 1) < HEAD_DIM
        for n in range(2):
            cols = slice(n * 128, (n + 1) * 128)
            q = qkv[0, r * 128:(r + 1) * 128, cols]
            k = qkv[1, :span, cols]
            v = qkv[2, :span, cols]
            mixed = []
            for h in range(2):
                keep = first if h == 0 else jnp.logical_not(first)
                qh = jnp.where(keep, q.astype(F32), 0.0).astype(BF16)
                scores = lax.dot_general(qh, k, (((1,), (1,)), ((), ())), preferred_element_type=F32)
                scores = jnp.where(allowed, scores / math.sqrt(HEAD_DIM), MASKED)
                scores = jnp.exp(scores - jnp.max(scores, axis=-1, keepdims=True))
                weights = (scores / jnp.sum(scores, axis=-1, keepdims=True)).astype(BF16)
                mixed.append(jnp.dot(weights, v, preferred_element_type=F32))
            att[r * 128:(r + 1) * 128, cols] = jnp.where(first, mixed[0], mixed[1]).astype(BF16)

    parts_in[2].wait()

    def project(n, carry):
        cols = pl.ds(pl.multiple_of(n * 256, 256), 256)
        part = jnp.dot(att[...], ow_ref[:, cols], preferred_element_type=F32)
        pb[:, :, cols] = part.astype(BF16).reshape(8, TOK, 256)
        return carry

    lax.fori_loop(0, D // 256, project, 0)

    def land(k):
        return r1.at[k] if k < 2 else (rz if k == 6 else r2.at[k - 2])

    back = Gather(lambda dx, dz: pb.at[inner_slot(dx, dz)], land, inner_devices, (psem_s, psem_r), 0)
    back.start(0, 1, 4, 5)

    ship(7)
    def settle(k, carry):
        s = lax.rem(me + k, 128)
        remote(rbuf.at[s], rbuf.at[s], gsend.at[s], grecv.at[s], (s // 8, s % 8)).wait_recv()
        return carry

    wt[:, 352:384, :] = jnp.zeros((2, 32, D), BF16)
    parts_in[3].wait()
    dw_ref[FFL:] = jnp.zeros((FFP - FFL, D), BF16)


    flat = rbuf.reshape(128 * ROWS, 2, FFL)

    def turn_step(n, carry):
        cols = pl.ds(pl.multiple_of(n * 256, 256), 256)
        wt[:, :FFL, cols] = jnp.transpose(flat[cols], (1, 2, 0))
        return carry

    back.middle()
    back.cross()
    resid_ref[...] = tok_ref[...].astype(F32) + back.total()

    residual = resid_ref[...]
    normed = normalize(residual, mgain_ref[...]).astype(BF16)
    logits = lax.dot_general(normed, rt_ref[...], (((1,), (1,)), ((), ())), preferred_element_type=F32)
    lanes = lax.broadcasted_iota(jnp.int32, (TOK, 8), 1)
    hot = [(ids_ref[:, n:n + 1] == lanes).astype(F32) for n in range(2)]
    chosen = [jnp.sum(h * logits, axis=-1, keepdims=True) for h in hot]
    first_weight = jax.nn.sigmoid(chosen[0] - chosen[1])
    before = lax.broadcasted_iota(jnp.int32, (TOK, TOK), 1) < lax.broadcasted_iota(jnp.int32, (TOK, TOK), 0)
    ranks = jnp.dot(before.astype(BF16), (hot[0] + hot[1]).astype(BF16), preferred_element_type=F32)
    base = (lanes * CAP).astype(F32)
    slots = lax.broadcasted_iota(jnp.int32, (TOK, 8 * CAP), 1).astype(F32)
    pick = [(jnp.sum(h * (base + ranks), axis=-1, keepdims=True) == slots).astype(F32) for h in hot]
    rows = lax.dot_general(
        (pick[0] + pick[1]).astype(BF16), normed, (((0,), (0,)), ((), ())), preferred_element_type=F32
    )
    asend[...] = rows.reshape(8, CAP // 2, 2, D).astype(BF16)
    def out_send(k):
        t = lax.rem(i + k, 8)
        return remote(asend.at[t], arecv.at[k], asem_s.at[k], asem_r.at[k], (g, t))

    core_copies = [
        remote(wt, wo, esem_s.at[0], esem_r.at[0], other_core),
        remote(dw_ref, dwo, esem_s.at[1], esem_r.at[1], other_core),
    ]

    devices = group_devices
    place = {(0, 0): (0, 0), (0, 1): (0, 1), (2, 0): (1, 0), (2, 1): (1, 1), (1, 0): (2, 0), (1, 1): (2, 1),
             (3, 0): (3, 0), (3, 1): (3, 1)}

    def make(cc):
        def block(ref):
            return lambda dx, dz: ref.at[(cc,) + place[(dx, dz)]]

        def land(k):
            return lands.at[cc, k]

        spread = RoutedSpread(block(xs), devices, (ysem_s, ysem_r), 9 * cc)
        gather = RoutedGather(block(ys), land, devices, (dsem_s, dsem_r), 8 * cc)
        return spread, gather

    spreads, gathers = zip(*[make(cc) for cc in range(NC)])

    for k in range(1, 8):
        out_send(k).start()
    arecv[0] = asend[i]
    lax.fori_loop(1, 128, settle, 0)
    lax.fori_loop(0, 5, turn_step, 0)
    for cc in range(NC):
        for k in range(4 * cc, 4 * cc + 4):
            if k:
                out_send(k).wait_recv()
        xs[cc, 0, 0] = arecv[4 * cc:4 * cc + 4].reshape(2 * CAP, 2, D).reshape(CH, D)
        spreads[cc].start(0, 1, 2)
    lax.fori_loop(5, 9, turn_step, 0)
    for copy in core_copies:
        copy.start()
    wt_copy = pltpu.make_async_copy(wt, wt_hbm, out_sem.at[1])
    wt_copy.start()

    def feed(cc, start, count):
        m = count * 2 * CH

        def up(t, carry):
            r = pl.ds(pl.multiple_of(t * 128, 128), 128)
            rows_in = xs[cc, start:start + count].reshape(m, D)
            for n, ref in enumerate((wt, wo)):
                both = jnp.concatenate([ref[0, r, :], ref[1, r, :]], axis=0)
                parts = lax.dot_general(rows_in, both, (((1,), (1,)), ((), ())), preferred_element_type=F32)
                hidden = jax.nn.silu(parts[:, :128]) * parts[:, 128:]
                hs[:m, pl.ds(pl.multiple_of(n * FFP + t * 128, 128), 128)] = hidden.astype(BF16)
            return carry

        lax.fori_loop(0, 3, up, 0)

        def down(n, carry):
            cols = pl.ds(pl.multiple_of(n * 256, 256), 256)
            part = jnp.dot(hs[:m, :FFP], dw_ref[:, cols], preferred_element_type=F32)
            part = part + jnp.dot(hs[:m, FFP:], dwo[:, cols], preferred_element_type=F32)
            ys[cc, start:start + count, :, :, cols] = part.astype(BF16).reshape(count, 2, CH, 256)
            return carry

        lax.fori_loop(0, D // 256, down, 0)

    def back_send(k):
        s = lax.rem(i + 8 - k, 8)
        return remote(bsend.at[k], brecv.at[i], bsem_s.at[k], bsem_r.at[k], (g, s))

    def finish(cc):
        bsend[4 * cc:4 * cc + 4] = gathers[cc].total().reshape(4, CAP // 2, 2, D).astype(BF16)
        for k in range(4 * cc, 4 * cc + 4):
            if k:
                back_send(k).start()
            else:
                brecv[i] = bsend[0]

    spreads[0].arrived(2)
    spreads[0].start(3, 4)
    spreads[1].arrived(2)
    spreads[1].start(3, 4)
    spreads[0].arrived(0)
    spreads[0].start(5)
    spreads[0].arrived(1)
    spreads[0].start(6)
    spreads[1].arrived(0)
    spreads[1].start(5)
    spreads[1].arrived(1)
    spreads[1].start(6)
    spreads[0].arrived(5)
    spreads[0].start(7)
    spreads[0].arrived(6)
    spreads[0].start(8)
    for copy in core_copies:
        copy.wait_recv()
    feed(0,  0, 1)
    spreads[1].arrived(5)
    spreads[1].start(7)
    spreads[1].arrived(6)
    spreads[1].start(8)
    spreads[0].arrived(3, 4)
    feed(0,  2, 2)
    gathers[0].start(5, 6)
    spreads[0].arrived(7, 8)
    feed(0,  1, 1)
    gathers[0].start(0)
    spreads[1].arrived(7, 8)
    feed(1,  1, 1)
    gathers[1].start(0)
    gathers[0].far()
    spreads[1].arrived(3, 4)
    feed(1,  2, 2)
    gathers[1].start(5, 6)
    gathers[1].far()
    gathers[0].middle()
    feed(1,  0, 1)
    gathers[1].middle()
    gathers[0].cross()
    gathers[1].cross()
    finish(0)
    finish(1)

    own_places = i * TOK + lax.broadcasted_iota(jnp.int32, (TOK, 1), 0)
    live = own_places < len_ref[0]
    for k in range(1, 8):
        e = lax.rem(i + k, 8)
        remote(brecv.at[e], brecv.at[e], bsem_s.at[k], bsem_r.at[k], (g, e)).wait_recv()
    flat = brecv[...].reshape(4 * CAP, 2, D).reshape(8 * CAP, D)
    first_out = jnp.dot(pick[0].astype(BF16), flat, preferred_element_type=F32)
    second_out = jnp.dot(pick[1].astype(BF16), flat, preferred_element_type=F32)
    combined = resid_ref[...] + (first_weight * first_out + (1.0 - first_weight) * second_out)
    out_ref[...] = jnp.where(live, combined, 0.0).astype(BF16)

    for k in range(1, 8):
        out_send(k).wait_send()
        back_send(k).wait_send()
    for copy in core_copies:
        copy.wait_send()
    for cc in range(NC):
        spreads[cc].drain()
        gathers[cc].drain()

    def sent(k, carry):
        t = lax.rem(me + k, 128)
        gate_send(t // 8, t % 8).wait_send()
        return carry

    lax.fori_loop(1, 128, sent, 0)
    for k in range(1, 8):
        slab_send(k).wait_send()
    tokens_all.drain()
    proj_all.drain()
    back.drain()
    for k, (dx, dz) in enumerate(order):
        core_send(k, dx, dz).wait_send()
    q3_copy.wait()
    wt_copy.wait()


def layer(tokens, lengths, cuts, gain, freqs, tq, ow, gu, mgain, rt, ids, dw):
    vm = pl.BlockSpec(memory_space=pltpu.VMEM)
    sm = pl.BlockSpec(memory_space=pltpu.SMEM)
    hbm = pl.BlockSpec(memory_space=pl.ANY)
    dma = pltpu.SemaphoreType.DMA
    return pl.pallas_call(
        layer_kernel,
        name="layer",
        out_shape=(
            jax.ShapeDtypeStruct((TOK, D), BF16),
            jax.ShapeDtypeStruct((3, 16, 144, 256), BF16),
            jax.ShapeDtypeStruct((2, FFP, D), BF16),
        ),
        in_specs=[sm, sm, vm, vm, vm, vm, vm, hbm, hbm, hbm, hbm, hbm],
        out_specs=(vm, hbm, hbm),
        scratch_shapes=[
            pltpu.VMEM((TOK, D), BF16),
            pltpu.VMEM((ROWS, 3, 2048), F32),
            pltpu.VMEM((256, D), BF16),
            pltpu.VMEM((FFP, D), BF16),
            pltpu.VMEM((TOK, D), F32),
            pltpu.VMEM((2, ROWS, 2, 5760), F32),
            pltpu.VMEM((128, ROWS, 2, FFL), BF16),
            pltpu.VMEM((128, ROWS, 2, FFL), BF16),
            pltpu.VMEM((8, 9, 2, 768), BF16),
            pltpu.VMEM((8, 9, 2, 768), BF16),
            pltpu.VMEM((3, 16, 144, 256), BF16),
            pltpu.VMEM((8, TOK, D), BF16),
            pltpu.VMEM((3, SEQ, 256), BF16),
            pltpu.VMEM((SEQ, 256), BF16),
            pltpu.VMEM((8, TOK, D), BF16),
            pltpu.VMEM((2, TOK, D), BF16),
            pltpu.VMEM((4, TOK, D), BF16),
            pltpu.VMEM((TOK, D), BF16),
            pltpu.VMEM((2, FFP, D), BF16),
            pltpu.VMEM((8, CAP // 2, 2, D), BF16),
            pltpu.VMEM((8, CAP // 2, 2, D), BF16),
            pltpu.VMEM((8, CAP // 2, 2, D), BF16),
            pltpu.VMEM((8, CAP // 2, 2, D), BF16),
            pltpu.VMEM((NC, 4, 2, CH, D), BF16),
            pltpu.VMEM((NC, 4, 2, CH, D), BF16),
            pltpu.VMEM((NC, 7, CH, D), BF16),
            pltpu.VMEM((4 * CH, 2 * FFP), BF16),
            pltpu.VMEM((2, FFP, D), BF16),
            pltpu.VMEM((FFP, D), BF16),
            dma((4,)), dma((8,)), dma((128,)), dma((128,)), dma((8,)), dma((8,)), dma((7,)), dma((7,)),
            dma((7,)), dma((7,)), dma((8,)), dma((8,)), dma((7,)), dma((7,)), dma((2,)),
            dma((8,)), dma((8,)), dma((8,)), dma((8,)), dma((9 * NC,)), dma((9 * NC,)),
            dma((8 * NC,)), dma((8 * NC,)), dma((2,)), dma((2,)),
        ],
        compiler_params=pltpu.CompilerParams(collective_id=0, has_side_effects=True, vmem_limit_bytes=60 << 20),
    )(lengths, cuts, gain, freqs, mgain, rt, ids, tokens, tq, ow, dw, gu)


def body(
    tokens,
    lengths,
    tenant_cut,
    expert_ids,
    trainer_qkv,
    trainer_gate_up,
    out_weight,
    down_weight,
    attn_gain,
    moe_gain,
    router,
):
    half = HEAD_DIM // 2
    freqs = jnp.exp(-math.log(10000.0) * jnp.arange(half, dtype=F32) / half)
    freqs = jnp.tile(freqs, 4)[None, :]
    layer_out, q3, wt = layer(
        tokens[0], lengths, tenant_cut, attn_gain[None, :], freqs, trainer_qkv, out_weight, trainer_gate_up,
        moe_gain[None, :], router.T, expert_ids[0], down_weight[0],
    )
    server_qkv = jnp.transpose(q3.reshape(3, D, 256), (1, 0, 2))
    server_gate_up = jnp.transpose(wt[:, :FFL, :], (2, 0, 1))[None]
    return (server_qkv, server_gate_up, layer_out[None])


def solution(mesh):
    placed = (
        P("group", "inner", None),
        P("group"),
        P("group"),
        P("group", "inner", None),
        P(("group", "inner"), None, None),
        P(None, ("group", "inner"), None, None),
        P("inner", None),
        P("inner", "group", None),
        P(),
        P(),
        P(),
    )
    return jax.shard_map(
        body,
        mesh=mesh,
        in_specs=placed,
        out_specs=(
            P(None, None, "inner"),
            P("inner", None, None, "group"),
            P("group", "inner", None),
        ),
        check_vma=False,
    )
```

time: 276 us -> 248 us (0.90)
  Pallas kernels: 263 us -> 235 us
    pallas_call x2 -> x1, Pallas kernels: 263 us -> 235 us  [layer(): pl.pallas_call(layer_kernel, name='layer', out_shape=(jax.ShapeDtypeStruc...]
    unnamed x20 -> x6, local copies, waits for them, and re-layouts: 7.45 us -> 2.51 us
where the time goes in v2:
time: 248 us
  Pallas kernels  235 us (95%)
  local copies, waits for them, and re-layouts  11.2 us (5%)
    pallas_call x1, Pallas kernels, layer(): pl.pallas_call(layer_kernel, name='layer', out_shape=(jax.ShapeDtypeStruc...  235 us

profile of v2, /device:TPU:8, one launch (start us, length us, event | category | flops | bytes accessed | tf_op | source)
XLA Modules:
  0.0 247.6 jit_solution(8270791632540866133)
XLA Ops:
  1.9 0.6 broadcast_in_dim_tile.3.freq_ref
  2.6 1.3 broadcast_in_dim.12.gain_ref
  3.9 1.3 broadcast_in_dim.13.mgain_ref
  5.2 1.4 copy.14.ids_ref
  6.6 234.5 %layer.1 = (bf16[64,2304]{1,0:T(8,128)(2,1)}, bf16[3,16,144,256]{3,2,1,0:T(8,128)(2,1)}, bf16[2,384,2304]{2,1,0:T(8,128)(2,1)}) custom-call(s32[1]{0:T(128)S(6)} %copy.17.len_ref, s32[1]{0:T(128)S(6)} %copy.18.cut_ref, f32[1,2304]{1,0:T(1,128)} %broadcast_in_dim.12.gain_ref, f32[1,128]{1,0:T(1,128)} %broadcast_in_dim_tile.3.freq_ref, ...), custom_call_target="tpu_custom_call" | custom-call | tf_op jit(solution)/shard_map/layer/pallas_call | solution.py:659
  241.1 0.0 copy-start
  241.1 4.0 %slice_bitcast_fusion = bf16[1,2304,2,360]{1,3,2,0:T(8,128)(2,1)} fusion(bf16[2,384,2304]{2,1,0:T(8,128)(2,1)} %get-tuple-element.7), kind=kLoop, calls=%fused_computation | loop fusion | bytes 6635520 | tf_op jit(solution)/shard_map/broadcast_in_dim | solution.py:729
  245.1 0.0 copy-done
  245.1 0.0 copy-start.1
  245.1 1.8 copy.19
  246.9 0.0 copy-done.1
  246.9 0.7 copy.20
  (2 shorter events, 0.0 us)
Async XLA Ops:
  241.1 4.0 %copy-start = (bf16[3,16,144,256]{3,2,1,0:T(8,128)(2,1)S(1)}, bf16[3,16,144,256]{3,2,1,0:T(8,128)(2,1)}, u32[]{:S(2)}) copy-start(bf16[3,16,144,256]{3,2,1,0:T(8,128)(2,1)} %get-tuple-element.6) | copy-start | bytes 10616836
  245.1 1.8 copy-start.1

commit v3 on v2

--- a/solution.py
+++ b/solution.py
@@ -322,7 +322,7 @@
             load(k + 2).start()
 
         def post(q, carry):
-            tg = lax.rem(g + q, 16)
+            tg = lax.rem(g + 5 * q, 16)
             gate_send(tg, e).start()
             return carry
 
@@ -519,19 +519,14 @@
     for k in range(1, 8):
         out_send(k).start()
     arecv[0] = asend[i]
-    lax.fori_loop(1, 128, settle, 0)
-    lax.fori_loop(0, 5, turn_step, 0)
     for cc in range(NC):
         for k in range(4 * cc, 4 * cc + 4):
             if k:
                 out_send(k).wait_recv()
         xs[cc, 0, 0] = arecv[4 * cc:4 * cc + 4].reshape(2 * CAP, 2, D).reshape(CH, D)
         spreads[cc].start(0, 1, 2)
-    lax.fori_loop(5, 9, turn_step, 0)
-    for copy in core_copies:
-        copy.start()
-    wt_copy = pltpu.make_async_copy(wt, wt_hbm, out_sem.at[1])
-    wt_copy.start()
+    lax.fori_loop(1, 128, settle, 0)
+    lax.fori_loop(0, 5, turn_step, 0)
 
     def feed(cc, start, count):
         m = count * 2 * CH
@@ -571,12 +566,17 @@
 
     spreads[0].arrived(2)
     spreads[0].start(3, 4)
-    spreads[1].arrived(2)
-    spreads[1].start(3, 4)
+    lax.fori_loop(5, 9, turn_step, 0)
+    for copy in core_copies:
+        copy.start()
+    wt_copy = pltpu.make_async_copy(wt, wt_hbm, out_sem.at[1])
+    wt_copy.start()
     spreads[0].arrived(0)
     spreads[0].start(5)
     spreads[0].arrived(1)
     spreads[0].start(6)
+    spreads[1].arrived(2)
+    spreads[1].start(3, 4)
     spreads[1].arrived(0)
     spreads[1].start(5)
     spreads[1].arrived(1)

time: 248 us -> 247 us (level)
  no operation moved by 1% of the time
where the time goes in v3:
time: 247 us
  Pallas kernels  234 us (95%)
  local copies, waits for them, and re-layouts  11.2 us (5%)
    pallas_call x1, Pallas kernels, layer(): pl.pallas_call(layer_kernel, name='layer', out_shape=(jax.ShapeDtypeStruc...  234 us

profile of v3, /device:TPU:8, one launch (start us, length us, event | category | flops | bytes accessed | tf_op | source)
XLA Modules:
  0.0 246.8 jit_solution(17156243535199555663)
XLA Ops:
  1.9 0.6 broadcast_in_dim_tile.3.freq_ref
  2.6 1.3 broadcast_in_dim.12.gain_ref
  3.9 1.3 broadcast_in_dim.13.mgain_ref
  5.2 1.4 copy.14.ids_ref
  6.6 233.7 %layer.1 = (bf16[64,2304]{1,0:T(8,128)(2,1)}, bf16[3,16,144,256]{3,2,1,0:T(8,128)(2,1)}, bf16[2,384,2304]{2,1,0:T(8,128)(2,1)}) custom-call(s32[1]{0:T(128)S(6)} %copy.17.len_ref, s32[1]{0:T(128)S(6)} %copy.18.cut_ref, f32[1,2304]{1,0:T(1,128)} %broadcast_in_dim.12.gain_ref, f32[1,128]{1,0:T(1,128)} %broadcast_in_dim_tile.3.freq_ref, ...), custom_call_target="tpu_custom_call" | custom-call | tf_op jit(solution)/shard_map/layer/pallas_call | solution.py:659
  240.3 0.0 copy-start
  240.3 4.0 %slice_bitcast_fusion = bf16[1,2304,2,360]{1,3,2,0:T(8,128)(2,1)} fusion(bf16[2,384,2304]{2,1,0:T(8,128)(2,1)} %get-tuple-element.7), kind=kLoop, calls=%fused_computation | loop fusion | bytes 6635520 | tf_op jit(solution)/shard_map/broadcast_in_dim | solution.py:729
  244.3 0.0 copy-done
  244.3 0.0 copy-start.1
  244.3 1.8 copy.19
  246.1 0.0 copy-done.1
  246.1 0.7 copy.20
  (2 shorter events, 0.0 us)
Async XLA Ops:
  240.3 4.0 %copy-start = (bf16[3,16,144,256]{3,2,1,0:T(8,128)(2,1)S(1)}, bf16[3,16,144,256]{3,2,1,0:T(8,128)(2,1)}, u32[]{:S(2)}) copy-start(bf16[3,16,144,256]{3,2,1,0:T(8,128)(2,1)} %get-tuple-element.6) | copy-start | bytes 10616836
  244.3 1.8 copy-start.1
